TPU v7x, 256 devices: a whole 4x4x8 slice. The times are simulated.
256 devices in a mesh: dom: 64 (over x, z, core), slab: 4 (over y).
Axes of the slice: x: 4, y: 4, z: 8, core: 2. Of those that a mesh axis runs over, the one named last changes fastest.
Arguments:
- logperm: float32 [256, 16, 64, 128], P('dom', 'slab'), may hold values from -4.2 to 4.2
- source: float32 [16, 64, 128], P('slab'), may hold values from -6 to 6
- observed: float32 [16, 64, 128], P('slab'), may hold values from -1.2 to 1.2
- brownian: float32 [256, 256], replicated, may hold values from -6 to 6
Outputs:
- particles_next: float32 [256, 16, 64, 128], P('dom', 'slab')
All inputs are finite; a program needn't handle non-finite values.
Results may differ from a plain program's by a relative error of at most 0.0003.
Values sent between devices are 32-bit elements; how exact they have to be, the bound alone decides.
No kernel may reach another device: no remote copies, remote signals or barrier semaphores. Data moves between devices by JAX's collectives and lax.ppermute only.
A program may use at most 64 MiB of HBM per device.

v0:
```python
import math
import jax
import jax.numpy as jnp
from jax import lax
from jax.sharding import PartitionSpec as P

SWEEPS = 8
misfit_weight = 1000.0


def with_halo(block, sides, width):
    for axis, dim in sides:
        count = lax.axis_size(axis)
        forward = [(i, i + 1) for i in range(count - 1)]
        backward = [(target, source) for source, target in forward]
        low = lax.ppermute(
            lax.slice_in_dim(block, block.shape[dim] - width, None, axis=dim), axis, forward
        )
        high = lax.ppermute(lax.slice_in_dim(block, 0, width, axis=dim), axis, backward)
        block = jnp.concatenate([low, block, high], axis=dim)
    return block


def neighbor_sum(core, below, above, fill):
    pad_y = jnp.pad(core, ((0, 0), (0, 0), (1, 1), (0, 0)), constant_values=fill)
    pad_z = jnp.pad(core, ((0, 0), (0, 0), (0, 0), (1, 1)), constant_values=fill)
    return below + above + pad_y[:, :, :-2] + pad_y[:, :, 2:] + pad_z[..., :-2] + pad_z[..., 2:]


def grad_field(e_core, e_below, e_above, p_core, p_below, p_above, q_core, q_below, q_above):
    summed = e_below * (p_core - p_below) * (q_core - q_below) + e_above * (p_core - p_above) * (
        q_core - q_above
    )
    for dimension in (2, 3):
        padding = [(0, 0), (0, 0), (0, 0), (0, 0)]
        padding[dimension] = (1, 1)
        e_pad = jnp.pad(e_core, padding, constant_values=1.0)
        p_pad = jnp.pad(p_core, padding)
        q_pad = jnp.pad(q_core, padding)
        extent = e_core.shape[dimension]
        for offset in (0, 2):
            e_near = lax.slice_in_dim(e_pad, offset, offset + extent, axis=dimension)
            p_near = lax.slice_in_dim(p_pad, offset, offset + extent, axis=dimension)
            q_near = lax.slice_in_dim(q_pad, offset, offset + extent, axis=dimension)
            summed = summed + e_near * (p_core - p_near) * (q_core - q_near)
    return -0.5 * e_core * summed


def on_device(logperm, source, observed, brownian):
    particles, width, rows_y, depth_z = logperm.shape
    slabs = lax.axis_size("slab")
    cells = width * slabs * rows_y * depth_z
    extended = with_halo(logperm, (("slab", 1),), 1)
    e_ext = jnp.exp(0.5 * extended)
    e_core = e_ext[:, 1:-1]
    inverse = 1.0 / neighbor_sum(e_core, e_ext[:, :-2], e_ext[:, 2:], 1.0)

    def relax_rim(rhs):
        value = inverse * rhs
        for sweep_index in range(SWEEPS - 1):
            bordered = with_halo(value, (("slab", 1),), 1)
            value = inverse * (
                rhs + e_core * neighbor_sum(value, bordered[:, :-2], bordered[:, 2:], 0.0)
            )
        return value / e_core

    pressure = relax_rim(source[None])
    misfit = misfit_weight * (pressure - observed[None])
    adjoint = relax_rim(misfit)
    states = with_halo(jnp.stack([pressure, adjoint]), (("slab", 2),), 1)
    gradient = grad_field(
        e_core,
        e_ext[:, :-2],
        e_ext[:, 2:],
        pressure,
        states[0][:, :-2],
        states[0][:, 2:],
        adjoint,
        states[1][:, :-2],
        states[1][:, 2:],
    )
    g_flat = gradient.reshape(particles, -1)
    u_cells, g_cells = (
        lax.all_to_all(
            logperm.reshape(particles, -1), "dom", split_axis=1, concat_axis=0, tiled=True
        ),
        lax.all_to_all(g_flat, "dom", split_axis=1, concat_axis=0, tiled=True),
    )
    ensemble = u_cells.shape[0]
    centre = jnp.mean(u_cells, axis=0, keepdims=True)
    spread = u_cells - centre
    partial_gram = lax.dot_general(
        spread,
        g_cells,
        (((1,), (1,)), ((), ())),
        precision=lax.Precision.HIGHEST,
        preferred_element_type=jnp.float32,
    )
    gram = lax.psum(partial_gram, ("dom", "slab"))
    step_size = ensemble / (4.0 * (cells + 1))
    mixing = -(step_size / ensemble) * gram + math.sqrt(2.0 * step_size / ensemble) * brownian
    moved = (
        centre
        + 1.25 * spread
        + lax.dot_general(
            mixing,
            spread,
            (((0,), (0,)), ((), ())),
            precision=lax.Precision.HIGHEST,
            preferred_element_type=jnp.float32,
        )
    )
    returned = lax.all_to_all(moved, "dom", split_axis=0, concat_axis=1, tiled=True)
    return returned.reshape(logperm.shape)


def solution(mesh):
    return jax.shard_map(
        on_device,
        mesh=mesh,
        in_specs=(P("dom", "slab", None, None), P("slab", None, None), P("slab", None, None), P()),
        out_specs=P("dom", "slab", None, None),
        check_vma=False,
    )
```

profile of v0, /device:TPU:1, one launch (start us, length us, event | category | flops | bytes accessed | tf_op | source)
XLA Modules:
  0.0 498.0 jit_solution(12891519340523834035)
XLA Ops:
  7.6 4.0 collective-permute-start
  13.7 3.6 collective-permute-done.1
  18.9 3.2 collective-permute-start.2
  24.1 3.8 collective-permute-done.3
  28.3 2.9 collective-permute-start.4
  33.1 3.8 collective-permute-done.5
  37.3 2.2 collective-permute-start.6
  41.5 3.8 collective-permute-done.7
  49.5 3.8 collective-permute-done.9
  57.6 3.8 collective-permute-done.11
  61.8 2.1 collective-permute-start.12
  66.1 4.1 collective-permute-done.13
  75.3 3.9 collective-permute-done.15
  79.7 2.1 collective-permute-start.16
  84.2 3.8 collective-permute-done.17
  88.4 2.2 collective-permute-start.18
  92.6 3.8 collective-permute-done.19
  96.9 2.2 collective-permute-start.20
  101.0 3.8 collective-permute-done.21
  105.3 2.2 collective-permute-start.22
  109.4 3.8 collective-permute-done.23
  113.7 1.9 collective-permute-start.24
  117.5 3.8 collective-permute-done.25
  125.7 3.8 collective-permute-done.27
  133.8 3.9 collective-permute-done.29
  139.1 2.6 collective-permute-start.30
  144.2 28.9 %all-to-all-start = ((f32[4,64,512]{2,0,1:T(4,128)}), f32[4,64,512]{2,0,1:T(4,128)S(1)}, u32[]{:S(2)}, u32[]{:S(2)}) async-start(f32[4,64,512]{2,0,1:T(4,128)} %copy.7), calls=%async_computation | async-start | bytes 1048576 | tf_op jit(solution)/shard_map/all_to_all | solution.py:84
  176.8 13.7 %all-to-all-done = f32[4,64,512]{2,0,1:T(4,128)S(1)} async-done(((f32[4,64,512]{2,0,1:T(4,128)}), f32[4,64,512]{2,0,1:T(4,128)S(1)}, u32[]{:S(2)}, u32[]{:S(2)}) %all-to-all-start) | async-done | bytes 524320 | tf_op jit(solution)/shard_map/all_to_all | solution.py:84
  190.4 6.3 %all-to-all-start.1 = ((f32[4,64,512]{2,0,1:T(4,128)}), f32[4,64,512]{2,0,1:T(4,128)S(1)}, u32[]{:S(2)}, u32[]{:S(2)}) async-start(f32[4,64,512]{2,0,1:T(4,128)} %copy.8), calls=%async_computation.1 | async-start | bytes 1048576 | tf_op jit(solution)/shard_map/all_to_all | solution.py:87
  197.2 16.9 %all-to-all-done.1 = f32[4,64,512]{2,0,1:T(4,128)S(1)} async-done(((f32[4,64,512]{2,0,1:T(4,128)}), f32[4,64,512]{2,0,1:T(4,128)S(1)}, u32[]{:S(2)}, u32[]{:S(2)}) %all-to-all-start.1) | async-done | bytes 524320 | tf_op jit(solution)/shard_map/all_to_all | solution.py:87
  215.8 245.4 %all-reduce.36.cloned.1.call-done = f32[256,256]{1,0:T(8,128)} async-done(((f32[256,256]{1,0:T(8,128)}), f32[256,256]{1,0:T(8,128)}) %all-reduce.36.cloned.1.call-update) | async-done | bytes 262160 | tf_op jit(solution)/shard_map/psum | solution.py:99
  462.9 27.3 %all_to_all.54 = f32[64,4,512]{2,1,0:T(4,128)S(1)} all-to-all(f32[64,4,512]{2,1,0:T(4,128)S(1)} %all_to_all.48), channel_id=1, replica_groups=mesh['dom'=64,'slab'=4] {'dom'}, dimensions={0} | all-to-all | bytes 1048576 | tf_op jit(solution)/shard_map/all_to_all | solution.py:113
  (99 shorter events, 60.8 us)
Async XLA Ops:
  7.6 6.2 %collective-permute-start = (f32[4,1,64,128]{3,2,1,0:T(8,128)S(1)}, f32[4,1,64,128]{3,2,1,0:T(8,128)S(1)}, u32[]{:S(2)}, u32[]{:S(2)}) collective-permute-start(f32[4,1,64,128]{3,2,1,0:T(8,128)S(1)} %get-tuple-element.41), channel_id=1, source_target_pairs={{0,1},{1,2},{2,3},{4,5},{5,6},{6,7},{8,9},{9,10},{10,11},{12,13},{... | collective-permute-start | bytes 393224 | tf_op jit(solution)/shard_map/ppermute | solution.py:16
  11.6 5.7 %collective-permute-start.1 = (f32[4,1,64,128]{3,2,1,0:T(8,128)S(1)}, f32[4,1,64,128]{3,2,1,0:T(8,128)S(1)}, u32[]{:S(2)}, u32[]{:S(2)}) collective-permute-start(f32[4,1,64,128]{3,2,1,0:T(8,128)S(1)} %get-tuple-element.42), channel_id=1, source_target_pairs={{1,0},{2,1},{3,2},{5,4},{6,5},{7,6},{9,8},{10,9},{11,10},{13,12},{... | collective-permute-start | bytes 393224 | tf_op jit(solution)/shard_map/ppermute | solution.py:19
  18.9 5.1 %collective-permute-start.2 = (f32[4,1,64,128]{3,2,1,0:T(8,128)S(1)}, f32[4,1,64,128]{3,2,1,0:T(8,128)S(1)}, u32[]{:S(2)}, u32[]{:S(2)}) collective-permute-start(f32[4,1,64,128]{3,2,1,0:T(8,128)S(1)} %get-tuple-element.39), channel_id=1, source_target_pairs={{0,1},{1,2},{2,3},{4,5},{5,6},{6,7},{8,9},{9,10},{10,11},{12,13},{... | collective-permute-start | bytes 393224 | tf_op jit(solution)/shard_map/ppermute | solution.py:16
  22.2 5.7 %collective-permute-start.3 = (f32[4,1,64,128]{3,2,1,0:T(8,128)S(1)}, f32[4,1,64,128]{3,2,1,0:T(8,128)S(1)}, u32[]{:S(2)}, u32[]{:S(2)}) collective-permute-start(f32[4,1,64,128]{3,2,1,0:T(8,128)S(1)} %get-tuple-element.40), channel_id=1, source_target_pairs={{1,0},{2,1},{3,2},{5,4},{6,5},{7,6},{9,8},{10,9},{11,10},{13,12},{... | collective-permute-start | bytes 393224 | tf_op jit(solution)/shard_map/ppermute | solution.py:19
  28.3 4.8 collective-permute-start.4
  31.2 5.7 %collective-permute-start.5 = (f32[4,1,64,128]{3,2,1,0:T(8,128)S(1)}, f32[4,1,64,128]{3,2,1,0:T(8,128)S(1)}, u32[]{:S(2)}, u32[]{:S(2)}) collective-permute-start(f32[4,1,64,128]{3,2,1,0:T(8,128)S(1)} %get-tuple-element.38), channel_id=1, source_target_pairs={{1,0},{2,1},{3,2},{5,4},{6,5},{7,6},{9,8},{10,9},{11,10},{13,12},{... | collective-permute-start | bytes 393224 | tf_op jit(solution)/shard_map/ppermute | solution.py:19
  37.3 4.1 collective-permute-start.6
  39.6 5.7 %collective-permute-start.7 = (f32[4,1,64,128]{3,2,1,0:T(8,128)S(1)}, f32[4,1,64,128]{3,2,1,0:T(8,128)S(1)}, u32[]{:S(2)}, u32[]{:S(2)}) collective-permute-start(f32[4,1,64,128]{3,2,1,0:T(8,128)S(1)} %get-tuple-element.36), channel_id=1, source_target_pairs={{1,0},{2,1},{3,2},{5,4},{6,5},{7,6},{9,8},{10,9},{11,10},{13,12},{... | collective-permute-start | bytes 393224 | tf_op jit(solution)/shard_map/ppermute | solution.py:19
  47.6 5.7 %collective-permute-start.9 = (f32[4,1,64,128]{3,2,1,0:T(8,128)S(1)}, f32[4,1,64,128]{3,2,1,0:T(8,128)S(1)}, u32[]{:S(2)}, u32[]{:S(2)}) collective-permute-start(f32[4,1,64,128]{3,2,1,0:T(8,128)S(1)} %get-tuple-element.34), channel_id=1, source_target_pairs={{1,0},{2,1},{3,2},{5,4},{6,5},{7,6},{9,8},{10,9},{11,10},{13,12},{... | collective-permute-start | bytes 393224 | tf_op jit(solution)/shard_map/ppermute | solution.py:19
  53.7 3.9 collective-permute-start.10
  55.7 5.7 %collective-permute-start.11 = (f32[4,1,64,128]{3,2,1,0:T(8,128)S(1)}, f32[4,1,64,128]{3,2,1,0:T(8,128)S(1)}, u32[]{:S(2)}, u32[]{:S(2)}) collective-permute-start(f32[4,1,64,128]{3,2,1,0:T(8,128)S(1)} %get-tuple-element.32), channel_id=1, source_target_pairs={{1,0},{2,1},{3,2},{5,4},{6,5},{7,6},{9,8},{10,9},{11,10},{13,12},{... | collective-permute-start | bytes 393224 | tf_op jit(solution)/shard_map/ppermute | solution.py:19
  61.8 4.3 collective-permute-start.12
  63.9 6.3 %collective-permute-start.13 = (f32[4,1,64,128]{3,2,1,0:T(8,128)S(1)}, f32[4,1,64,128]{3,2,1,0:T(8,128)S(1)}, u32[]{:S(2)}, u32[]{:S(2)}) collective-permute-start(f32[4,1,64,128]{3,2,1,0:T(8,128)S(1)} %get-tuple-element.30), channel_id=1, source_target_pairs={{1,0},{2,1},{3,2},{5,4},{6,5},{7,6},{9,8},{10,9},{11,10},{13,12},{... | collective-permute-start | bytes 393224 | tf_op jit(solution)/shard_map/ppermute | solution.py:19
  70.6 4.7 collective-permute-start.14
  72.3 7.0 %collective-permute-start.15 = (f32[4,1,64,128]{3,2,1,0:T(8,128)S(1)}, f32[4,1,64,128]{3,2,1,0:T(8,128)S(1)}, u32[]{:S(2)}, u32[]{:S(2)}) collective-permute-start(f32[4,1,64,128]{3,2,1,0:T(8,128)S(1)} %get-tuple-element.28), channel_id=1, source_target_pairs={{1,0},{2,1},{3,2},{5,4},{6,5},{7,6},{9,8},{10,9},{11,10},{13,12},{... | collective-permute-start | bytes 393224 | tf_op jit(solution)/shard_map/ppermute | solution.py:19
  79.7 4.4 collective-permute-start.16
  81.9 6.1 %collective-permute-start.17 = (f32[4,1,64,128]{3,2,1,0:T(8,128)S(1)}, f32[4,1,64,128]{3,2,1,0:T(8,128)S(1)}, u32[]{:S(2)}, u32[]{:S(2)}) collective-permute-start(f32[4,1,64,128]{3,2,1,0:T(8,128)S(1)} %get-tuple-element.26), channel_id=1, source_target_pairs={{1,0},{2,1},{3,2},{5,4},{6,5},{7,6},{9,8},{10,9},{11,10},{13,12},{... | collective-permute-start | bytes 393224 | tf_op jit(solution)/shard_map/ppermute | solution.py:19
  88.4 4.2 collective-permute-start.18
  90.7 5.7 %collective-permute-start.19 = (f32[4,1,64,128]{3,2,1,0:T(8,128)S(1)}, f32[4,1,64,128]{3,2,1,0:T(8,128)S(1)}, u32[]{:S(2)}, u32[]{:S(2)}) collective-permute-start(f32[4,1,64,128]{3,2,1,0:T(8,128)S(1)} %get-tuple-element.24), channel_id=1, source_target_pairs={{1,0},{2,1},{3,2},{5,4},{6,5},{7,6},{9,8},{10,9},{11,10},{13,12},{... | collective-permute-start | bytes 393224 | tf_op jit(solution)/shard_map/ppermute | solution.py:19
  96.9 4.1 collective-permute-start.20
  99.1 5.7 %collective-permute-start.21 = (f32[4,1,64,128]{3,2,1,0:T(8,128)S(1)}, f32[4,1,64,128]{3,2,1,0:T(8,128)S(1)}, u32[]{:S(2)}, u32[]{:S(2)}) collective-permute-start(f32[4,1,64,128]{3,2,1,0:T(8,128)S(1)} %get-tuple-element.22), channel_id=1, source_target_pairs={{1,0},{2,1},{3,2},{5,4},{6,5},{7,6},{9,8},{10,9},{11,10},{13,12},{... | collective-permute-start | bytes 393224 | tf_op jit(solution)/shard_map/ppermute | solution.py:19
  105.3 4.1 collective-permute-start.22
  107.5 5.7 %collective-permute-start.23 = (f32[4,1,64,128]{3,2,1,0:T(8,128)S(1)}, f32[4,1,64,128]{3,2,1,0:T(8,128)S(1)}, u32[]{:S(2)}, u32[]{:S(2)}) collective-permute-start(f32[4,1,64,128]{3,2,1,0:T(8,128)S(1)} %get-tuple-element.20), channel_id=1, source_target_pairs={{1,0},{2,1},{3,2},{5,4},{6,5},{7,6},{9,8},{10,9},{11,10},{13,12},{... | collective-permute-start | bytes 393224 | tf_op jit(solution)/shard_map/ppermute | solution.py:19
  113.7 3.9 collective-permute-start.24
  115.6 5.7 %collective-permute-start.25 = (f32[4,1,64,128]{3,2,1,0:T(8,128)S(1)}, f32[4,1,64,128]{3,2,1,0:T(8,128)S(1)}, u32[]{:S(2)}, u32[]{:S(2)}) collective-permute-start(f32[4,1,64,128]{3,2,1,0:T(8,128)S(1)} %get-tuple-element.18), channel_id=1, source_target_pairs={{1,0},{2,1},{3,2},{5,4},{6,5},{7,6},{9,8},{10,9},{11,10},{13,12},{... | collective-permute-start | bytes 393224 | tf_op jit(solution)/shard_map/ppermute | solution.py:19
  123.8 5.7 %collective-permute-start.27 = (f32[4,1,64,128]{3,2,1,0:T(8,128)S(1)}, f32[4,1,64,128]{3,2,1,0:T(8,128)S(1)}, u32[]{:S(2)}, u32[]{:S(2)}) collective-permute-start(f32[4,1,64,128]{3,2,1,0:T(8,128)S(1)} %get-tuple-element.16), channel_id=1, source_target_pairs={{1,0},{2,1},{3,2},{5,4},{6,5},{7,6},{9,8},{10,9},{11,10},{13,12},{... | collective-permute-start | bytes 393224 | tf_op jit(solution)/shard_map/ppermute | solution.py:19
  131.9 5.8 %collective-permute-start.29 = (f32[4,1,64,128]{3,2,1,0:T(8,128)S(1)}, f32[4,1,64,128]{3,2,1,0:T(8,128)S(1)}, u32[]{:S(2)}, u32[]{:S(2)}) collective-permute-start(f32[4,1,64,128]{3,2,1,0:T(8,128)S(1)} %get-tuple-element.14), channel_id=1, source_target_pairs={{1,0},{2,1},{3,2},{5,4},{6,5},{7,6},{9,8},{10,9},{11,10},{13,12},{... | collective-permute-start | bytes 393224 | tf_op jit(solution)/shard_map/ppermute | solution.py:19
  139.1 34.0 %collective-permute-start.30 = (f32[2,4,1,64,128]{4,3,2,1,0:T(8,128)}, f32[2,4,1,64,128]{4,3,2,1,0:T(8,128)}, u32[]{:S(2)}, u32[]{:S(2)}) collective-permute-start(f32[2,4,1,64,128]{4,3,2,1,0:T(8,128)} %get-tuple-element.11), channel_id=1, source_target_pairs={{0,1},{1,2},{2,3},{4,5},{5,6},{6,7},{8,9},{9,10},{10,11},{12,13},{... | collective-permute-start | bytes 786440 | tf_op jit(solution)/shard_map/ppermute | solution.py:16
  141.7 31.4 %collective-permute-start.31 = (f32[2,4,1,64,128]{4,3,2,1,0:T(8,128)}, f32[2,4,1,64,128]{4,3,2,1,0:T(8,128)}, u32[]{:S(2)}, u32[]{:S(2)}) collective-permute-start(f32[2,4,1,64,128]{4,3,2,1,0:T(8,128)} %get-tuple-element.12), channel_id=1, source_target_pairs={{1,0},{2,1},{3,2},{5,4},{6,5},{7,6},{9,8},{10,9},{11,10},{13,12},{... | collective-permute-start | bytes 786440 | tf_op jit(solution)/shard_map/ppermute | solution.py:19
  144.2 46.2 %all-to-all-start = ((f32[4,64,512]{2,0,1:T(4,128)}), f32[4,64,512]{2,0,1:T(4,128)S(1)}, u32[]{:S(2)}, u32[]{:S(2)}) async-start(f32[4,64,512]{2,0,1:T(4,128)} %copy.7), calls=%async_computation | async-start | bytes 1048576 | tf_op jit(solution)/shard_map/all_to_all | solution.py:84
  190.4 23.6 %all-to-all-start.1 = ((f32[4,64,512]{2,0,1:T(4,128)}), f32[4,64,512]{2,0,1:T(4,128)S(1)}, u32[]{:S(2)}, u32[]{:S(2)}) async-start(f32[4,64,512]{2,0,1:T(4,128)} %copy.8), calls=%async_computation.1 | async-start | bytes 1048576 | tf_op jit(solution)/shard_map/all_to_all | solution.py:87
  196.7 264.4 %all-reduce.36.cloned.1.call-start = ((), (), s32[]{:S(2)}) async-start(), calls=%async_computation.3 | async-start | bytes 524288 | tf_op jit(solution)/shard_map/psum | solution.py:99
  (7 other events, 299.0 us)
Sparse Core Ops, SparseCore 0:
  215.7 245.3 all-reduce.35
where the time goes:
time: 499 us; the launch traced here: 498 us
  waiting for transfers between devices  344 us (69%)
  starting transfers between devices  93 us (19%)
  blocking collectives  27.3 us (5%)
  between operations  14.1 us (3%)
  other arithmetic  10.8 us (2%)
  local copies, waits for them, and re-layouts  5.66 us (1%)
    psum x1, waiting for transfers between devices, on_device(): gram = lax.psum(partial_gram, ('dom', 'slab'))  245 us
    ppermute x16, waiting for transfers between devices, with_halo(): lax.ppermute(lax.slice_in_dim(block, 0, width, axis=dim), axis, backward)  57.2 us
    ppermute x16, starting transfers between devices, with_halo(): lax.ppermute(lax.slice_in_dim(block, block.shape[dim] - width, None, axis...  37 us
    all_to_all x1, starting transfers between devices, on_device(): lax.all_to_all(logperm.reshape(particles, -1), 'dom', split_axis=1, conca...  28.9 us
    all_to_all x1, blocking collectives, on_device(): lax.all_to_all(moved, 'dom', split_axis=0, concat_axis=1, tiled=True)  27.3 us
    ppermute x16, starting transfers between devices, with_halo(): lax.ppermute(lax.slice_in_dim(block, 0, width, axis=dim), axis, backward)  20.8 us
    all_to_all x1, waiting for transfers between devices, on_device(): lax.all_to_all(g_flat, 'dom', split_axis=1, concat_axis=0, tiled=True)  16.9 us
    all_to_all x1, waiting for transfers between devices, on_device(): lax.all_to_all(logperm.reshape(particles, -1), 'dom', split_axis=1, conca...  13.7 us
  transfers between devices with their start and end apart: 35, of which 33 were waited for; matrix products, arithmetic and copies ran while one was open for 1% of the time, Pallas kernels for 0%

commit v1 on v0

--- a/solution.py
+++ b/solution.py
@@ -96,7 +96,7 @@
         precision=lax.Precision.HIGHEST,
         preferred_element_type=jnp.float32,
     )
-    gram = lax.psum(partial_gram, ("dom", "slab"))
+    gram = lax.psum(lax.psum(partial_gram, axis_name="dom"), axis_name="slab")
     step_size = ensemble / (4.0 * (cells + 1))
     mixing = -(step_size / ensemble) * gram + math.sqrt(2.0 * step_size / ensemble) * brownian
     moved = (

time: 499 us -> 473 us (0.948)
  waiting for transfers between devices: 344 us -> 315 us
    psum x1 -> x2, waiting for transfers between devices: 245 us -> 216 us  [on_device(): gram = lax.psum(lax.psum(partial_gram, axis_name='dom'), axis_name='slab')]
  transfers between devices with their start and end apart: 35 -> 36, of which waited for: 33 -> 34; matrix products, arithmetic and copies ran while one was open for 1% -> 1% of each run, Pallas kernels for 0% -> 0%
where the time goes in v1:
time: 473 us; the launch traced here: 472 us
  waiting for transfers between devices  315 us (67%)
  starting transfers between devices  93 us (20%)
  blocking collectives  29.9 us (6%)
  between operations  14.1 us (3%)
  other arithmetic  10.8 us (2%)
  local copies, waits for them, and re-layouts  5.66 us (1%)
    psum x2, waiting for transfers between devices, on_device(): gram = lax.psum(lax.psum(partial_gram, axis_name='dom'), axis_name='slab')  216 us
    ppermute x16, waiting for transfers between devices, with_halo(): lax.ppermute(lax.slice_in_dim(block, 0, width, axis=dim), axis, backward)  57.2 us
    ppermute x16, starting transfers between devices, with_halo(): lax.ppermute(lax.slice_in_dim(block, block.shape[dim] - width, None, axis...  37 us
    all_to_all x1, blocking collectives, on_device(): lax.all_to_all(moved, 'dom', split_axis=0, concat_axis=1, tiled=True)  29.9 us
    all_to_all x1, starting transfers between devices, on_device(): lax.all_to_all(logperm.reshape(particles, -1), 'dom', split_axis=1, conca...  28.9 us
    ppermute x16, starting transfers between devices, with_halo(): lax.ppermute(lax.slice_in_dim(block, 0, width, axis=dim), axis, backward)  20.8 us
    all_to_all x1, waiting for transfers between devices, on_device(): lax.all_to_all(g_flat, 'dom', split_axis=1, concat_axis=0, tiled=True)  16.9 us
    all_to_all x1, waiting for transfers between devices, on_device(): lax.all_to_all(logperm.reshape(particles, -1), 'dom', split_axis=1, conca...  13.7 us
  transfers between devices with their start and end apart: 36, of which 34 were waited for; matrix products, arithmetic and copies ran while one was open for 1% of the time, Pallas kernels for 0%

profile of v1, /device:TPU:1, one launch (start us, length us, event | category | flops | bytes accessed | tf_op | source)
XLA Modules:
  0.0 471.7 jit_solution(7714318694255793960)
XLA Ops:
  7.6 4.0 collective-permute-start
  13.7 3.6 collective-permute-done.1
  18.9 3.2 collective-permute-start.2
  24.1 3.8 collective-permute-done.3
  28.3 2.9 collective-permute-start.4
  33.1 3.8 collective-permute-done.5
  37.3 2.2 collective-permute-start.6
  41.5 3.8 collective-permute-done.7
  49.5 3.8 collective-permute-done.9
  57.6 3.8 collective-permute-done.11
  61.8 2.1 collective-permute-start.12
  66.1 4.1 collective-permute-done.13
  75.3 3.9 collective-permute-done.15
  79.7 2.1 collective-permute-start.16
  84.2 3.8 collective-permute-done.17
  88.4 2.2 collective-permute-start.18
  92.6 3.8 collective-permute-done.19
  96.9 2.2 collective-permute-start.20
  101.0 3.8 collective-permute-done.21
  105.3 2.2 collective-permute-start.22
  109.4 3.8 collective-permute-done.23
  117.5 3.8 collective-permute-done.25
  125.7 3.8 collective-permute-done.27
  133.8 3.9 collective-permute-done.29
  139.1 2.6 collective-permute-start.30
  144.2 28.9 %all-to-all-start = ((f32[4,64,512]{2,0,1:T(4,128)}), f32[4,64,512]{2,0,1:T(4,128)S(1)}, u32[]{:S(2)}, u32[]{:S(2)}) async-start(f32[4,64,512]{2,0,1:T(4,128)} %copy.7), calls=%async_computation | async-start | bytes 1048576 | tf_op jit(solution)/shard_map/all_to_all | solution.py:84
  176.8 13.7 %all-to-all-done = f32[4,64,512]{2,0,1:T(4,128)S(1)} async-done(((f32[4,64,512]{2,0,1:T(4,128)}), f32[4,64,512]{2,0,1:T(4,128)S(1)}, u32[]{:S(2)}, u32[]{:S(2)}) %all-to-all-start) | async-done | bytes 524320 | tf_op jit(solution)/shard_map/all_to_all | solution.py:84
  190.4 6.3 %all-to-all-start.1 = ((f32[4,64,512]{2,0,1:T(4,128)}), f32[4,64,512]{2,0,1:T(4,128)S(1)}, u32[]{:S(2)}, u32[]{:S(2)}) async-start(f32[4,64,512]{2,0,1:T(4,128)} %copy.8), calls=%async_computation.1 | async-start | bytes 1048576 | tf_op jit(solution)/shard_map/all_to_all | solution.py:87
  197.2 16.9 %all-to-all-done.1 = f32[4,64,512]{2,0,1:T(4,128)S(1)} async-done(((f32[4,64,512]{2,0,1:T(4,128)}), f32[4,64,512]{2,0,1:T(4,128)S(1)}, u32[]{:S(2)}, u32[]{:S(2)}) %all-to-all-start.1) | async-done | bytes 524320 | tf_op jit(solution)/shard_map/all_to_all | solution.py:87
  215.6 172.2 %all-reduce.37.cloned.1.call-done = f32[256,256]{1,0:T(8,128)} async-done(((f32[256,256]{1,0:T(8,128)}), f32[256,256]{1,0:T(8,128)}) %all-reduce.37.cloned.1.call-update) | async-done | bytes 262160 | tf_op jit(solution)/shard_map/psum | solution.py:99
  388.0 44.1 %all-reduce.39.cloned.1.call-done = f32[256,256]{1,0:T(8,128)} async-done(((f32[256,256]{1,0:T(8,128)}), f32[256,256]{1,0:T(8,128)}) %all-reduce.39.cloned.1.call-update) | async-done | bytes 262160 | tf_op jit(solution)/shard_map/psum | solution.py:99
  433.9 29.9 %all_to_all.54 = f32[64,4,512]{2,1,0:T(4,128)S(1)} all-to-all(f32[64,4,512]{2,1,0:T(4,128)S(1)} %all_to_all.48), channel_id=1, replica_groups=mesh['dom'=64,'slab'=4] {'dom'}, dimensions={0} | all-to-all | bytes 1048576 | tf_op jit(solution)/shard_map/all_to_all | solution.py:113
  (102 shorter events, 62.8 us)
Async XLA Ops:
  7.6 6.2 %collective-permute-start = (f32[4,1,64,128]{3,2,1,0:T(8,128)S(1)}, f32[4,1,64,128]{3,2,1,0:T(8,128)S(1)}, u32[]{:S(2)}, u32[]{:S(2)}) collective-permute-start(f32[4,1,64,128]{3,2,1,0:T(8,128)S(1)} %get-tuple-element.41), channel_id=1, source_target_pairs={{0,1},{1,2},{2,3},{4,5},{5,6},{6,7},{8,9},{9,10},{10,11},{12,13},{... | collective-permute-start | bytes 393224 | tf_op jit(solution)/shard_map/ppermute | solution.py:16
  11.6 5.7 %collective-permute-start.1 = (f32[4,1,64,128]{3,2,1,0:T(8,128)S(1)}, f32[4,1,64,128]{3,2,1,0:T(8,128)S(1)}, u32[]{:S(2)}, u32[]{:S(2)}) collective-permute-start(f32[4,1,64,128]{3,2,1,0:T(8,128)S(1)} %get-tuple-element.42), channel_id=1, source_target_pairs={{1,0},{2,1},{3,2},{5,4},{6,5},{7,6},{9,8},{10,9},{11,10},{13,12},{... | collective-permute-start | bytes 393224 | tf_op jit(solution)/shard_map/ppermute | solution.py:19
  18.9 5.1 %collective-permute-start.2 = (f32[4,1,64,128]{3,2,1,0:T(8,128)S(1)}, f32[4,1,64,128]{3,2,1,0:T(8,128)S(1)}, u32[]{:S(2)}, u32[]{:S(2)}) collective-permute-start(f32[4,1,64,128]{3,2,1,0:T(8,128)S(1)} %get-tuple-element.39), channel_id=1, source_target_pairs={{0,1},{1,2},{2,3},{4,5},{5,6},{6,7},{8,9},{9,10},{10,11},{12,13},{... | collective-permute-start | bytes 393224 | tf_op jit(solution)/shard_map/ppermute | solution.py:16
  22.2 5.7 %collective-permute-start.3 = (f32[4,1,64,128]{3,2,1,0:T(8,128)S(1)}, f32[4,1,64,128]{3,2,1,0:T(8,128)S(1)}, u32[]{:S(2)}, u32[]{:S(2)}) collective-permute-start(f32[4,1,64,128]{3,2,1,0:T(8,128)S(1)} %get-tuple-element.40), channel_id=1, source_target_pairs={{1,0},{2,1},{3,2},{5,4},{6,5},{7,6},{9,8},{10,9},{11,10},{13,12},{... | collective-permute-start | bytes 393224 | tf_op jit(solution)/shard_map/ppermute | solution.py:19
  28.3 4.8 %collective-permute-start.4 = (f32[4,1,64,128]{3,2,1,0:T(8,128)S(1)}, f32[4,1,64,128]{3,2,1,0:T(8,128)S(1)}, u32[]{:S(2)}, u32[]{:S(2)}) collective-permute-start(f32[4,1,64,128]{3,2,1,0:T(8,128)S(1)} %get-tuple-element.37), channel_id=1, source_target_pairs={{0,1},{1,2},{2,3},{4,5},{5,6},{6,7},{8,9},{9,10},{10,11},{12,13},{... | collective-permute-start | bytes 393224 | tf_op jit(solution)/shard_map/ppermute | solution.py:16
  31.2 5.7 %collective-permute-start.5 = (f32[4,1,64,128]{3,2,1,0:T(8,128)S(1)}, f32[4,1,64,128]{3,2,1,0:T(8,128)S(1)}, u32[]{:S(2)}, u32[]{:S(2)}) collective-permute-start(f32[4,1,64,128]{3,2,1,0:T(8,128)S(1)} %get-tuple-element.38), channel_id=1, source_target_pairs={{1,0},{2,1},{3,2},{5,4},{6,5},{7,6},{9,8},{10,9},{11,10},{13,12},{... | collective-permute-start | bytes 393224 | tf_op jit(solution)/shard_map/ppermute | solution.py:19
  37.3 4.1 collective-permute-start.6
  39.6 5.7 %collective-permute-start.7 = (f32[4,1,64,128]{3,2,1,0:T(8,128)S(1)}, f32[4,1,64,128]{3,2,1,0:T(8,128)S(1)}, u32[]{:S(2)}, u32[]{:S(2)}) collective-permute-start(f32[4,1,64,128]{3,2,1,0:T(8,128)S(1)} %get-tuple-element.36), channel_id=1, source_target_pairs={{1,0},{2,1},{3,2},{5,4},{6,5},{7,6},{9,8},{10,9},{11,10},{13,12},{... | collective-permute-start | bytes 393224 | tf_op jit(solution)/shard_map/ppermute | solution.py:19
  47.6 5.7 %collective-permute-start.9 = (f32[4,1,64,128]{3,2,1,0:T(8,128)S(1)}, f32[4,1,64,128]{3,2,1,0:T(8,128)S(1)}, u32[]{:S(2)}, u32[]{:S(2)}) collective-permute-start(f32[4,1,64,128]{3,2,1,0:T(8,128)S(1)} %get-tuple-element.34), channel_id=1, source_target_pairs={{1,0},{2,1},{3,2},{5,4},{6,5},{7,6},{9,8},{10,9},{11,10},{13,12},{... | collective-permute-start | bytes 393224 | tf_op jit(solution)/shard_map/ppermute | solution.py:19
  53.7 3.9 collective-permute-start.10
  55.7 5.7 %collective-permute-start.11 = (f32[4,1,64,128]{3,2,1,0:T(8,128)S(1)}, f32[4,1,64,128]{3,2,1,0:T(8,128)S(1)}, u32[]{:S(2)}, u32[]{:S(2)}) collective-permute-start(f32[4,1,64,128]{3,2,1,0:T(8,128)S(1)} %get-tuple-element.32), channel_id=1, source_target_pairs={{1,0},{2,1},{3,2},{5,4},{6,5},{7,6},{9,8},{10,9},{11,10},{13,12},{... | collective-permute-start | bytes 393224 | tf_op jit(solution)/shard_map/ppermute | solution.py:19
  61.8 4.3 collective-permute-start.12
  63.9 6.3 %collective-permute-start.13 = (f32[4,1,64,128]{3,2,1,0:T(8,128)S(1)}, f32[4,1,64,128]{3,2,1,0:T(8,128)S(1)}, u32[]{:S(2)}, u32[]{:S(2)}) collective-permute-start(f32[4,1,64,128]{3,2,1,0:T(8,128)S(1)} %get-tuple-element.30), channel_id=1, source_target_pairs={{1,0},{2,1},{3,2},{5,4},{6,5},{7,6},{9,8},{10,9},{11,10},{13,12},{... | collective-permute-start | bytes 393224 | tf_op jit(solution)/shard_map/ppermute | solution.py:19
  70.6 4.7 collective-permute-start.14
  72.3 7.0 %collective-permute-start.15 = (f32[4,1,64,128]{3,2,1,0:T(8,128)S(1)}, f32[4,1,64,128]{3,2,1,0:T(8,128)S(1)}, u32[]{:S(2)}, u32[]{:S(2)}) collective-permute-start(f32[4,1,64,128]{3,2,1,0:T(8,128)S(1)} %get-tuple-element.28), channel_id=1, source_target_pairs={{1,0},{2,1},{3,2},{5,4},{6,5},{7,6},{9,8},{10,9},{11,10},{13,12},{... | collective-permute-start | bytes 393224 | tf_op jit(solution)/shard_map/ppermute | solution.py:19
  79.7 4.4 collective-permute-start.16
  81.9 6.1 %collective-permute-start.17 = (f32[4,1,64,128]{3,2,1,0:T(8,128)S(1)}, f32[4,1,64,128]{3,2,1,0:T(8,128)S(1)}, u32[]{:S(2)}, u32[]{:S(2)}) collective-permute-start(f32[4,1,64,128]{3,2,1,0:T(8,128)S(1)} %get-tuple-element.26), channel_id=1, source_target_pairs={{1,0},{2,1},{3,2},{5,4},{6,5},{7,6},{9,8},{10,9},{11,10},{13,12},{... | collective-permute-start | bytes 393224 | tf_op jit(solution)/shard_map/ppermute | solution.py:19
  88.4 4.2 collective-permute-start.18
  90.7 5.7 %collective-permute-start.19 = (f32[4,1,64,128]{3,2,1,0:T(8,128)S(1)}, f32[4,1,64,128]{3,2,1,0:T(8,128)S(1)}, u32[]{:S(2)}, u32[]{:S(2)}) collective-permute-start(f32[4,1,64,128]{3,2,1,0:T(8,128)S(1)} %get-tuple-element.24), channel_id=1, source_target_pairs={{1,0},{2,1},{3,2},{5,4},{6,5},{7,6},{9,8},{10,9},{11,10},{13,12},{... | collective-permute-start | bytes 393224 | tf_op jit(solution)/shard_map/ppermute | solution.py:19
  96.9 4.1 collective-permute-start.20
  99.1 5.7 %collective-permute-start.21 = (f32[4,1,64,128]{3,2,1,0:T(8,128)S(1)}, f32[4,1,64,128]{3,2,1,0:T(8,128)S(1)}, u32[]{:S(2)}, u32[]{:S(2)}) collective-permute-start(f32[4,1,64,128]{3,2,1,0:T(8,128)S(1)} %get-tuple-element.22), channel_id=1, source_target_pairs={{1,0},{2,1},{3,2},{5,4},{6,5},{7,6},{9,8},{10,9},{11,10},{13,12},{... | collective-permute-start | bytes 393224 | tf_op jit(solution)/shard_map/ppermute | solution.py:19
  105.3 4.1 collective-permute-start.22
  107.5 5.7 %collective-permute-start.23 = (f32[4,1,64,128]{3,2,1,0:T(8,128)S(1)}, f32[4,1,64,128]{3,2,1,0:T(8,128)S(1)}, u32[]{:S(2)}, u32[]{:S(2)}) collective-permute-start(f32[4,1,64,128]{3,2,1,0:T(8,128)S(1)} %get-tuple-element.20), channel_id=1, source_target_pairs={{1,0},{2,1},{3,2},{5,4},{6,5},{7,6},{9,8},{10,9},{11,10},{13,12},{... | collective-permute-start | bytes 393224 | tf_op jit(solution)/shard_map/ppermute | solution.py:19
  115.6 5.7 %collective-permute-start.25 = (f32[4,1,64,128]{3,2,1,0:T(8,128)S(1)}, f32[4,1,64,128]{3,2,1,0:T(8,128)S(1)}, u32[]{:S(2)}, u32[]{:S(2)}) collective-permute-start(f32[4,1,64,128]{3,2,1,0:T(8,128)S(1)} %get-tuple-element.18), channel_id=1, source_target_pairs={{1,0},{2,1},{3,2},{5,4},{6,5},{7,6},{9,8},{10,9},{11,10},{13,12},{... | collective-permute-start | bytes 393224 | tf_op jit(solution)/shard_map/ppermute | solution.py:19
  123.8 5.7 %collective-permute-start.27 = (f32[4,1,64,128]{3,2,1,0:T(8,128)S(1)}, f32[4,1,64,128]{3,2,1,0:T(8,128)S(1)}, u32[]{:S(2)}, u32[]{:S(2)}) collective-permute-start(f32[4,1,64,128]{3,2,1,0:T(8,128)S(1)} %get-tuple-element.16), channel_id=1, source_target_pairs={{1,0},{2,1},{3,2},{5,4},{6,5},{7,6},{9,8},{10,9},{11,10},{13,12},{... | collective-permute-start | bytes 393224 | tf_op jit(solution)/shard_map/ppermute | solution.py:19
  131.9 5.8 %collective-permute-start.29 = (f32[4,1,64,128]{3,2,1,0:T(8,128)S(1)}, f32[4,1,64,128]{3,2,1,0:T(8,128)S(1)}, u32[]{:S(2)}, u32[]{:S(2)}) collective-permute-start(f32[4,1,64,128]{3,2,1,0:T(8,128)S(1)} %get-tuple-element.14), channel_id=1, source_target_pairs={{1,0},{2,1},{3,2},{5,4},{6,5},{7,6},{9,8},{10,9},{11,10},{13,12},{... | collective-permute-start | bytes 393224 | tf_op jit(solution)/shard_map/ppermute | solution.py:19
  139.1 34.0 %collective-permute-start.30 = (f32[2,4,1,64,128]{4,3,2,1,0:T(8,128)}, f32[2,4,1,64,128]{4,3,2,1,0:T(8,128)}, u32[]{:S(2)}, u32[]{:S(2)}) collective-permute-start(f32[2,4,1,64,128]{4,3,2,1,0:T(8,128)} %get-tuple-element.11), channel_id=1, source_target_pairs={{0,1},{1,2},{2,3},{4,5},{5,6},{6,7},{8,9},{9,10},{10,11},{12,13},{... | collective-permute-start | bytes 786440 | tf_op jit(solution)/shard_map/ppermute | solution.py:16
  141.7 31.4 %collective-permute-start.31 = (f32[2,4,1,64,128]{4,3,2,1,0:T(8,128)}, f32[2,4,1,64,128]{4,3,2,1,0:T(8,128)}, u32[]{:S(2)}, u32[]{:S(2)}) collective-permute-start(f32[2,4,1,64,128]{4,3,2,1,0:T(8,128)} %get-tuple-element.12), channel_id=1, source_target_pairs={{1,0},{2,1},{3,2},{5,4},{6,5},{7,6},{9,8},{10,9},{11,10},{13,12},{... | collective-permute-start | bytes 786440 | tf_op jit(solution)/shard_map/ppermute | solution.py:19
  144.2 46.2 %all-to-all-start = ((f32[4,64,512]{2,0,1:T(4,128)}), f32[4,64,512]{2,0,1:T(4,128)S(1)}, u32[]{:S(2)}, u32[]{:S(2)}) async-start(f32[4,64,512]{2,0,1:T(4,128)} %copy.7), calls=%async_computation | async-start | bytes 1048576 | tf_op jit(solution)/shard_map/all_to_all | solution.py:84
  190.4 23.6 %all-to-all-start.1 = ((f32[4,64,512]{2,0,1:T(4,128)}), f32[4,64,512]{2,0,1:T(4,128)S(1)}, u32[]{:S(2)}, u32[]{:S(2)}) async-start(f32[4,64,512]{2,0,1:T(4,128)} %copy.8), calls=%async_computation.1 | async-start | bytes 1048576 | tf_op jit(solution)/shard_map/all_to_all | solution.py:87
  196.7 191.1 %all-reduce.37.cloned.1.call-start = ((), (), s32[]{:S(2)}) async-start(), calls=%async_computation.3 | async-start | bytes 524288 | tf_op jit(solution)/shard_map/psum | solution.py:99
  215.6 216.6 %all-reduce.39.cloned.1.call-start = ((), (), s32[]{:S(2)}) async-start(), calls=%async_computation.4 | async-start | bytes 524288 | tf_op jit(solution)/shard_map/psum | solution.py:99
  (8 other events, 273.9 us)
Sparse Core Ops, SparseCore 0:
  215.7 172.0 all-reduce.36
  390.2 41.8 all-reduce.38
